TPU v7x, 32 devices: a whole 2x2x4 slice. The times are simulated.
32 devices in a mesh: enc: 2 (over x), batch: 16 (over z, y, core).
Axes of the slice: x: 2, y: 2, z: 4, core: 2. Of those that a mesh axis runs over, the one named last changes fastest.
Arguments:
- tokens: bfloat16 [2, 16384, 768], P('enc', 'batch'), may hold values from -6 to 6
- cotangent: bfloat16 [2, 16384, 768], P('enc', 'batch'), may hold values from -6 to 6
- projection: bfloat16 [2, 768, 2304], P('enc'), may hold values from -0.21875 to 0.21875
- offsets: bfloat16 [2, 1536], P('enc'), may hold values from -1.1953125 to 1.1953125
- merger: bfloat16 [2, 768, 768], P('enc'), may hold values from -1.75 to 1.75
- adjust: bfloat16 [2, 768], P('enc'), may hold values from -1.1953125 to 1.1953125
- scaling: bfloat16 [2, 768], P('enc'), may hold values from 0.5 to 1.5
- centering: bfloat16 [2, 768], P('enc'), may hold values from -1.1953125 to 1.1953125
- expansion: bfloat16 [2, 768, 3072], P('enc'), may hold values from -0.21875 to 0.21875
- lifting: bfloat16 [2, 3072], P('enc'), may hold values from -1.1953125 to 1.1953125
- contraction: bfloat16 [2, 3072, 768], P('enc'), may hold values from -0.15625 to 0.15625
- settling: bfloat16 [2, 768], P('enc'), may hold values from -1.1953125 to 1.1953125
- rescale: bfloat16 [2, 768], P('enc'), may hold values from 0.5 to 1.5
- recenter: bfloat16 [2, 768], P('enc'), may hold values from -1.1953125 to 1.1953125
- segments: int32 [16384], P('batch'), may hold values from 0 to 15, as said below
- passage_starts: int32 [256], P('batch'), may hold values from 0 to 1023, as said below
- passage_counts: int32 [16], replicated, may hold values from 4 to 16, as said below
- positives: int32 [256], P('batch'), may hold values from 0 to 255, as said below
Outputs:
- encoded: bfloat16 [2, 16384, 768], P('enc', 'batch')
- tokens_gradient: float32 [2, 16384, 768], P('enc', 'batch')
- gradient_projection: float32 [2, 768, 2304], P('enc')
- gradient_offsets: float32 [2, 1536], P('enc')
- gradient_merger: float32 [2, 768, 768], P('enc')
- gradient_adjust: float32 [2, 768], P('enc')
- gradient_scaling: float32 [2, 768], P('enc')
- gradient_centering: float32 [2, 768], P('enc')
- gradient_expansion: float32 [2, 768, 3072], P('enc')
- gradient_lifting: float32 [2, 3072], P('enc')
- gradient_contraction: float32 [2, 3072, 768], P('enc')
- gradient_settling: float32 [2, 768], P('enc')
- gradient_rescale: float32 [2, 768], P('enc')
- gradient_recenter: float32 [2, 768], P('enc')
Inputs may be any that keep to these rules, and one draw needn't show every extreme that they name: `segments`: within one index of batch, passages are runs of consecutive tokens numbered from 0 upward in order; every row of 256 tokens starts a passage and holds 1 to 4 of them; passages start at multiples of 8. `passage_starts`: on each index of batch, slot s below that index's passage count holds the position of passage s's first token; other slots hold arbitrary positions. `passage_counts`: the number of passages on each index of batch; some index holds 16 in every draw. `positives`: A slot i * 16 + s with s below the passage count of index i.
All inputs are finite; a program needn't handle non-finite values.
Results may differ from a plain program's by a relative error of at most 0.014.
Values may be sent and summed in bfloat16 or wider, within the bound.
No kernel may reach another device: no remote copies, remote signals or barrier semaphores. Data moves between devices by JAX's collectives and lax.ppermute only.
A program may use at most 192 MiB of HBM per device.

v0:
```python
import math

import jax
import jax.numpy as jnp
from jax import lax
from jax.sharding import PartitionSpec as P

HEADS = 12
QLEN = 64
BLOCK = 512


EPSILON = 1e-12
SHARPNESS_DIVISOR = 2.0
LOSS_WEIGHT = 2.0
FLOAT_KIND = jnp.float32
BRAIN = jnp.bfloat16


def swapped(value, axis, apart):
    mask = 2**apart
    pairs = [(source, source ^ mask) for source in range(lax.axis_size(axis))]
    return lax.ppermute(value, axis, pairs)


def layer_norm(values, scale_row, shift_row):
    centered = values - jnp.mean(values, axis=-1, keepdims=True)
    spread = jnp.mean(centered * centered, axis=-1, keepdims=True)
    return centered * lax.rsqrt(spread + EPSILON) * scale_row + shift_row


def exact_gelu(values):
    return jax.nn.gelu(values, approximate=False)


def to_low(values):
    return values.astype(BRAIN)


def block_scores(queries, key_rows, block_marks):
    score_scale = 1.0 / math.sqrt(queries.shape[2])
    scores = (
        jnp.einsum("qhd,khd->hqk", queries, key_rows, preferred_element_type=FLOAT_KIND)
        * score_scale
    )
    same_mark = block_marks[:, None] == block_marks[None, :]
    return jnp.where(same_mark[None], scores, -1e30)


def attend_forward(parts):
    queries, key_rows, values, block_marks = parts
    scores = block_scores(queries, key_rows, block_marks)
    row_top = jnp.max(scores, axis=-1, keepdims=True)
    log_total = row_top + jnp.log(jnp.sum(jnp.exp(scores - row_top), axis=-1, keepdims=True))
    weights = to_low(jnp.exp(scores - log_total))
    context = jnp.einsum("hqk,khd->qhd", weights, values, preferred_element_type=FLOAT_KIND)
    return (to_low(context), log_total)


def attend_backward(parts):
    queries, key_rows, values, block_marks, log_total, gradient_context = parts
    score_scale = 1.0 / math.sqrt(queries.shape[2])
    probability = jnp.exp(block_scores(queries, key_rows, block_marks) - log_total)
    gradient_values = jnp.einsum(
        "hqk,qhd->khd", to_low(probability), gradient_context, preferred_element_type=FLOAT_KIND
    )
    gradient_probs = jnp.einsum(
        "qhd,khd->hqk", gradient_context, values, preferred_element_type=FLOAT_KIND
    )
    row_dots = jnp.sum(probability * gradient_probs, axis=-1, keepdims=True)
    gradient_scores = to_low(probability * (gradient_probs - row_dots))
    gradient_queries = (
        jnp.einsum("hqk,khd->qhd", gradient_scores, key_rows, preferred_element_type=FLOAT_KIND)
        * score_scale
    )
    gradient_keys = (
        jnp.einsum("hqk,qhd->khd", gradient_scores, queries, preferred_element_type=FLOAT_KIND)
        * score_scale
    )
    return (gradient_queries, gradient_keys, gradient_values)


def column_sums(values):
    return jnp.sum(values.astype(FLOAT_KIND), axis=0)


def logit_gradients(
    question_row_block, target_row_list, passage_row_block, valid_entries, smoothing_divisor
):
    score_matrix = (
        jnp.einsum(
            "qd,sd->qs", question_row_block, passage_row_block, preferred_element_type=FLOAT_KIND
        )
        * smoothing_divisor
    )
    score_matrix = jnp.where(valid_entries[None, :], score_matrix, -1e30)
    row_top = jnp.max(score_matrix, axis=1, keepdims=True)
    logit_total = row_top + jnp.log(jnp.sum(jnp.exp(score_matrix - row_top), axis=1, keepdims=True))
    probability = jnp.exp(score_matrix - logit_total)
    target_hit = (
        jnp.arange(score_matrix.shape[1], dtype=jnp.int32)[None, :] == target_row_list[:, None]
    )
    return to_low(LOSS_WEIGHT * (probability - target_hit.astype(FLOAT_KIND)))


def shards(
    tokens,
    cotangent,
    projection,
    offsets,
    merger,
    adjust,
    scaling,
    centering,
    expansion,
    lifting,
    contraction,
    settling,
    rescale,
    recenter,
    segments,
    passage_starts,
    passage_counts,
    positives,
):
    enc_index = lax.axis_index("enc")
    is_passage = enc_index == 1
    rows_in = tokens[0]
    row_count, feature_breadth = rows_in.shape
    head_count = HEADS
    head_size = feature_breadth // head_count
    block_count = row_count // BLOCK
    focus_weighting_array = projection[0]
    merge_matrix = merger[0]
    expand_matrix = expansion[0]
    shrink_matrix = contraction[0]
    offset_row = offsets[0].astype(FLOAT_KIND)
    adjust_row = adjust[0].astype(FLOAT_KIND)
    scaling_row = scaling[0].astype(FLOAT_KIND)
    centering_row = centering[0].astype(FLOAT_KIND)
    lifting_row = lifting[0].astype(FLOAT_KIND)
    settling_row = settling[0].astype(FLOAT_KIND)
    rescale_row = rescale[0].astype(FLOAT_KIND)
    recenter_row = recenter[0].astype(FLOAT_KIND)
    position = jnp.arange(row_count, dtype=jnp.int32)
    token_marks = jnp.where(is_passage, segments, position // QLEN)
    block_marks = token_marks.reshape(block_count, BLOCK)
    full_bias = jnp.concatenate(
        [
            offset_row[:feature_breadth],
            jnp.zeros((feature_breadth,), FLOAT_KIND),
            offset_row[feature_breadth:],
        ]
    )
    packed = to_low(
        jnp.dot(rows_in, focus_weighting_array, preferred_element_type=FLOAT_KIND) + full_bias
    )
    parted = packed.reshape(block_count, BLOCK, 3, head_count, head_size)
    queries = parted[:, :, 0]
    key_rows = parted[:, :, 1]
    values = parted[:, :, 2]
    context, log_total = lax.map(attend_forward, (queries, key_rows, values, block_marks))
    context = context.reshape(row_count, feature_breadth)
    attended = jnp.dot(context, merge_matrix, preferred_element_type=FLOAT_KIND) + adjust_row
    normed_one, first_back = jax.vjp(
        layer_norm, rows_in.astype(FLOAT_KIND) + attended, scaling_row, centering_row
    )
    first_low = to_low(normed_one)
    hidden = jnp.dot(first_low, expand_matrix, preferred_element_type=FLOAT_KIND) + lifting_row
    activated = to_low(exact_gelu(hidden))
    shrunk = jnp.dot(activated, shrink_matrix, preferred_element_type=FLOAT_KIND) + settling_row
    encoded, second_back = jax.vjp(layer_norm, normed_one + shrunk, rescale_row, recenter_row)
    encoded_low = to_low(encoded)
    slot_count = passage_starts.shape[0]
    half_count = slot_count // 2
    slot_index = jnp.arange(slot_count, dtype=jnp.int32)
    summary_rows = jnp.where(is_passage, passage_starts, slot_index * QLEN)
    picker = summary_rows[:, None] == position[None, :]
    summary_local = to_low(
        jnp.dot(picker.astype(BRAIN), encoded_low, preferred_element_type=FLOAT_KIND)
    )
    partner = swapped(summary_local, "enc", 0)
    passage_embedding = jnp.where(is_passage, summary_local, partner)
    question_embedding = jnp.where(is_passage, partner, summary_local)
    smoothing_divisor = SHARPNESS_DIVISOR / math.sqrt(feature_breadth)
    valid_entries = (slot_index[None, :] < passage_counts[:, None]).reshape(-1)
    collected_rows = lax.all_gather(passage_embedding, "batch", axis=0, tiled=True)
    local_questions = lax.dynamic_slice_in_dim(
        question_embedding, enc_index * half_count, half_count, 0
    )
    local_targets = lax.dynamic_slice_in_dim(positives, enc_index * half_count, half_count, 0)
    logits_gradient = logit_gradients(
        local_questions, local_targets, collected_rows, valid_entries, smoothing_divisor
    )
    gradient_questions = (
        jnp.dot(logits_gradient, collected_rows, preferred_element_type=FLOAT_KIND)
        * smoothing_divisor
    )
    gradient_passages = lax.psum_scatter(
        jnp.einsum("qs,qd->sd", logits_gradient, local_questions, preferred_element_type=FLOAT_KIND)
        * smoothing_divisor,
        "batch",
        scatter_dimension=0,
        tiled=True,
    )
    back_questions, back_passages = (
        swapped(gradient_questions.astype(jnp.bfloat16), "enc", 0).astype(gradient_questions.dtype),
        swapped(gradient_passages.astype(jnp.bfloat16), "enc", 0).astype(gradient_passages.dtype),
    )
    gradient_summary = jnp.where(
        is_passage,
        gradient_passages + back_passages,
        jnp.concatenate([gradient_questions, back_questions], axis=0),
    )
    gradient_encoded = cotangent[0].astype(FLOAT_KIND) + jnp.einsum(
        "ct,cd->td", picker.astype(FLOAT_KIND), gradient_summary, precision=lax.Precision.HIGHEST
    )
    gradient_two, gradient_rescale, gradient_recenter = second_back(gradient_encoded)
    gradient_shrunk = to_low(gradient_two)
    gradient_settling = column_sums(gradient_shrunk)
    gradient_contraction = jnp.einsum(
        "tf,td->fd", activated, gradient_shrunk, preferred_element_type=FLOAT_KIND
    )
    gradient_activated = jnp.einsum(
        "td,fd->tf", gradient_shrunk, shrink_matrix, preferred_element_type=FLOAT_KIND
    )
    gelu_again, gelu_back = jax.vjp(exact_gelu, hidden)
    gradient_hidden = to_low(gelu_back(gradient_activated)[0])
    gradient_lifting = column_sums(gradient_hidden)
    gradient_expansion = jnp.einsum(
        "td,tf->df", first_low, gradient_hidden, preferred_element_type=FLOAT_KIND
    )
    gradient_first = gradient_two + jnp.einsum(
        "tf,df->td", gradient_hidden, expand_matrix, preferred_element_type=FLOAT_KIND
    )
    gradient_one, gradient_scaling, gradient_centering = first_back(gradient_first)
    gradient_attended = to_low(gradient_one)
    gradient_adjust = column_sums(gradient_attended)
    gradient_merger = jnp.einsum(
        "tc,td->cd", context, gradient_attended, preferred_element_type=FLOAT_KIND
    )
    gradient_context = to_low(
        jnp.einsum("td,cd->tc", gradient_attended, merge_matrix, preferred_element_type=FLOAT_KIND)
    )
    gradient_context = gradient_context.reshape(block_count, BLOCK, head_count, head_size)
    gradient_queries, gradient_keys, gradient_values = lax.map(
        attend_backward, (queries, key_rows, values, block_marks, log_total, gradient_context)
    )
    gradient_packed = to_low(
        jnp.stack([gradient_queries, gradient_keys, gradient_values], axis=2).reshape(
            row_count, 3 * feature_breadth
        )
    )
    packed_sums = column_sums(gradient_packed)
    gradient_offsets = jnp.concatenate(
        [packed_sums[:feature_breadth], packed_sums[2 * feature_breadth :]]
    )
    gradient_projection = jnp.einsum(
        "td,te->de", rows_in, gradient_packed, preferred_element_type=FLOAT_KIND
    )
    tokens_gradient = gradient_one + jnp.einsum(
        "te,de->td", gradient_packed, focus_weighting_array, preferred_element_type=FLOAT_KIND
    )
    every_share = (
        lax.psum_scatter(gradient_projection, "batch", scatter_dimension=0, tiled=True),
        lax.psum_scatter(gradient_offsets, "batch", scatter_dimension=0, tiled=True),
        lax.psum_scatter(gradient_merger, "batch", scatter_dimension=0, tiled=True),
        lax.psum_scatter(gradient_adjust, "batch", scatter_dimension=0, tiled=True),
        lax.psum_scatter(gradient_scaling, "batch", scatter_dimension=0, tiled=True),
        lax.psum_scatter(gradient_centering, "batch", scatter_dimension=0, tiled=True),
        lax.psum_scatter(gradient_expansion, "batch", scatter_dimension=0, tiled=True),
        lax.psum_scatter(gradient_lifting, "batch", scatter_dimension=0, tiled=True),
        lax.psum_scatter(gradient_contraction, "batch", scatter_dimension=0, tiled=True),
        lax.psum_scatter(gradient_settling, "batch", scatter_dimension=0, tiled=True),
        lax.psum_scatter(gradient_rescale, "batch", scatter_dimension=0, tiled=True),
        lax.psum_scatter(gradient_recenter, "batch", scatter_dimension=0, tiled=True),
    )
    overall_aggregate = (
        lax.all_gather(every_share[0].astype(jnp.bfloat16), "batch", axis=0, tiled=True).astype(
            jnp.float32
        ),
        lax.all_gather(every_share[1].astype(jnp.bfloat16), "batch", axis=0, tiled=True).astype(
            jnp.float32
        ),
        lax.all_gather(every_share[2].astype(jnp.bfloat16), "batch", axis=0, tiled=True).astype(
            jnp.float32
        ),
        lax.all_gather(every_share[3].astype(jnp.bfloat16), "batch", axis=0, tiled=True).astype(
            jnp.float32
        ),
        lax.all_gather(every_share[4].astype(jnp.bfloat16), "batch", axis=0, tiled=True).astype(
            jnp.float32
        ),
        lax.all_gather(every_share[5].astype(jnp.bfloat16), "batch", axis=0, tiled=True).astype(
            jnp.float32
        ),
        lax.all_gather(every_share[6].astype(jnp.bfloat16), "batch", axis=0, tiled=True).astype(
            jnp.float32
        ),
        lax.all_gather(every_share[7].astype(jnp.bfloat16), "batch", axis=0, tiled=True).astype(
            jnp.float32
        ),
        lax.all_gather(every_share[8].astype(jnp.bfloat16), "batch", axis=0, tiled=True).astype(
            jnp.float32
        ),
        lax.all_gather(every_share[9].astype(jnp.bfloat16), "batch", axis=0, tiled=True).astype(
            jnp.float32
        ),
        lax.all_gather(every_share[10].astype(jnp.bfloat16), "batch", axis=0, tiled=True).astype(
            jnp.float32
        ),
        lax.all_gather(every_share[11].astype(jnp.bfloat16), "batch", axis=0, tiled=True).astype(
            jnp.float32
        ),
    )
    attend_total = overall_aggregate[:6]
    expand_total = overall_aggregate[6:]
    return (
        to_low(encoded)[None],
        tokens_gradient[None],
        attend_total[0][None],
        attend_total[1][None],
        attend_total[2][None],
        attend_total[3][None],
        attend_total[4][None],
        attend_total[5][None],
        expand_total[0][None],
        expand_total[1][None],
        expand_total[2][None],
        expand_total[3][None],
        expand_total[4][None],
        expand_total[5][None],
    )


def solution(mesh):
    return jax.shard_map(
        shards,
        mesh=mesh,
        in_specs=(
            P("enc", "batch", None),
            P("enc", "batch", None),
            P("enc", None, None),
            P("enc", None),
            P("enc", None, None),
            P("enc", None),
            P("enc", None),
            P("enc", None),
            P("enc", None, None),
            P("enc", None),
            P("enc", None, None),
            P("enc", None),
            P("enc", None),
            P("enc", None),
            P("batch"),
            P("batch"),
            P(),
            P("batch"),
        ),
        out_specs=(
            P("enc", "batch", None),
            P("enc", "batch", None),
            P("enc", None, None),
            P("enc", None),
            P("enc", None, None),
            P("enc", None),
            P("enc", None),
            P("enc", None),
            P("enc", None, None),
            P("enc", None),
            P("enc", None, None),
            P("enc", None),
            P("enc", None),
            P("enc", None),
        ),
        check_vma=False,
    )
```

profile of v0, /device:TPU:0, one launch (start us, length us, event | category | flops | bytes accessed | tf_op | source)
XLA Modules:
  0.0 909.1 jit_solution(17320595831040693999)
XLA Ops:
  14.7 7.3 add_convert_fusion.1
  22.0 6.6 copy.99
  28.6 8.8 reshape.236
  37.4 5.4 slice_bitcast_fusion
  47.3 26.4 %while.26 = (s32[]{:T(128)}, bf16[2,512,12,64]{1,3,2,0:T(8,128)(2,1)}, f32[2,12,512,1]{2,1,3,0:T(8,128)}, bf16[2,512,12,64]{1,3,2,0:T(8,128)(2,1)}, s32[2,512]{1...) while((s32[]{:T(128)}, ...), condition=%wide.region_3.4_spmd, body=%wide.region_0.3_spmd.sunk | while | flops 840558592 | bytes 43204736 | solution.py:162
  81.9 35.9 %multiply_convert_fusion.1 = (bf16[1024,3072]{1,0:T(8,128)(2,1)}, f32[1024,3072]{1,0:T(8,128)}, f32[1024,3072]{1,0:T(8,128)}) fusion(f32[3072]{0:T(1024)S(1)} %bitcast.227, bf16[1,768,3072]{2,1,0:T(8,128)(2,1)S(1)} %bitcast.233, f32[1024,768]{0,1:T(8,128)S(1)} %get-tuple-element.312, f32[768]{0:T(1024)S(1)} %get-tuple-element.324, ...), kind=kOutput, calls=%fused_computation.63 | convolution fusion | flops 5043388416 | bytes 39348224 | tf_op jit(solution)/shard_map/dot_general | solution.py:169
  117.9 7.7 fusion.99
  135.8 22.7 %all_gather.39 = bf16[256,768]{1,0:T(8,128)(2,1)S(1)} all-gather(bf16[16,768]{1,0:T(8,128)(2,1)S(1)} %broadcast_select_fusion), channel_id=1, replica_groups=mesh['enc'=2,'batch'=16] {'batch'}, dimensions={0}, use_global_device_ids=true | all-gather | bytes 417792 | tf_op jit(solution)/shard_map/all_gather | solution.py:187
  163.1 53.9 %reduce-scatter.8.cloned.1.call-done = f32[16,768]{1,0:T(8,128)} async-done(((f32[256,768]{1,0:T(8,128)}), f32[16,768]{1,0:T(8,128)}) %reduce-scatter.8.cloned.1.call-update) | async-done | bytes 49168 | tf_op jit(solution)/shard_map/reduce_scatter | solution.py:199
  226.5 5.8 multiply_reduce_fusion.1
  235.4 19.2 %convert_reduce_fusion = (f32[3072]{0:T(1024)}, bf16[1024,3072]{1,0:T(8,128)(2,1)}) fusion(f32[1024,3072]{1,0:T(8,128)} %get-tuple-element.299, bf16[1024,768]{0,1:T(8,128)(2,1)} %get-tuple-element.289, bf16[1,3072,768]{2,1,0:T(8,128)(2,1)} %param.32, f32[1024,3072]{1,0:T(8,128)} %get-tuple-element.313, f32[3072]{0:T(1024)S(1)} %bitcast.228), kind=kOutput, calls=%fused_computation.61 | convolution fusion | flops 4885312512 | bytes 37773312 | tf_op jit(solution)/shard_map/td,fd->tf/dot_general | solution.py:224
  254.7 11.2 %multiply_reduce_fusion.2 = (f32[768]{0:T(1024)}, f32[1024]{0:T(1024)S(1)}, f32[768]{0:T(1024)}, f32[1024,768]{0,1:T(8,128)S(1)}) fusion(f32[1024,768]{0,1:T(8,128)S(1)} %copy-done.10, f32[1024]{0:T(1024)S(1)} %copy-done.46, f32[1024]{0:T(1024)S(1)} %copy-done.35, f32[768]{0:T(1024)S(1)} %copy-done.42, bf16[1024,3072]{1,0:T(8,128)(2,1)} %get-tuple-element.323, ...), kind=kOutput, calls=%fused_computation.99 | convolution fusion | flops 4839699456 | bytes 20472832 | tf_op jit(solution)/shard_map/tf,df->td/dot_general | solution.py:233
  286.9 53.6 %while.27 = (s32[]{:T(128)}, bf16[2,512,12,64]{1,3,2,0:T(8,128)(2,1)}, bf16[2,512,12,64]{1,3,2,0:T(8,128)(2,1)}, bf16[2,512,12,64]{1,3,2,0:T(8,128)(2,1)}, bf16[...) while((s32[]{:T(128)}, ...), condition=%wide.region_17.18_spmd, body=%wide.region_15.17_spmd.sunk | while | flops 2061494272 | bytes 156175728 | solution.py:246
  295.3 6.8 multiply_reduce_fusion.8
  302.1 7.3 multiply_convert_fusion.6
  322.1 6.8 multiply_reduce_fusion.8
  328.9 7.2 multiply_convert_fusion.6
  345.5 9.4 %copy.112 = bf16[2,512,3,12,64]{1,0,4,3,2:T(2,128)(2,1)} copy(bf16[2,512,3,12,64]{1,4,3,0,2:T(8,128)(2,1)} %get-tuple-element.293) | data formatting | bytes 9437184 | tf_op jit(solution)/shard_map/stack | solution.py:250
  361.1 5.8 convolution_bitcast_fusion
  366.9 8.0 copy.124
  375.0 9.9 %fusion.103 = f32[3072,768]{1,0:T(8,128)} fusion(bf16[1024,3072]{1,0:T(8,128)(2,1)} %get-tuple-element.298, bf16[1024,768]{0,1:T(8,128)(2,1)} %get-tuple-element.289), kind=kOutput, calls=%fused_computation.197 | convolution fusion | flops 4831838208 | bytes 17301504 | tf_op jit(solution)/shard_map/tf,td->fd/dot_general | solution.py:221
  385.6 11.2 %fusion.90 = f32[768,3072]{1,0:T(8,128)} fusion(bf16[1024,3072]{1,0:T(8,128)(2,1)} %get-tuple-element.323, f32[1024,768]{0,1:T(8,128)} %copy-done.9, f32[768]{0:T(1024)S(1)} %copy-done.55, f32[768]{0:T(1024)S(1)} %copy-done.43, f32[1024]{0:T(1024)S(1)} %copy-done.47, f32[1024]{0:T(1024)S(1)} %copy-done.36), kind=kOutput, calls=%fused_computation.187 | convolution fusion | flops 4835770368 | bytes 18888704 | tf_op jit(solution)/shard_map/td,tf->df/dot_general | solution.py:230
  398.6 65.1 %reduce-scatter.16.cloned.1.call-done = f32[48,2304]{1,0:T(8,128)} async-done(((f32[768,2304]{1,0:T(8,128)}), f32[48,2304]{1,0:T(8,128)}) %reduce-scatter.16.cloned.1.call-update) | async-done | bytes 442384 | tf_op jit(solution)/shard_map/reduce_scatter | solution.py:265
  465.5 114.1 %reduce-scatter.14.cloned.1.call-done = f32[192,768]{1,0:T(8,128)} async-done(((f32[3072,768]{1,0:T(8,128)}), f32[192,768]{1,0:T(8,128)}) %reduce-scatter.14.cloned.1.call-update) | async-done | bytes 589840 | tf_op jit(solution)/shard_map/reduce_scatter | solution.py:273
  581.5 113.8 %reduce-scatter.12.cloned.1.call-done = f32[48,3072]{1,0:T(8,128)} async-done(((f32[768,3072]{1,0:T(8,128)}), f32[48,3072]{1,0:T(8,128)}) %reduce-scatter.12.cloned.1.call-update) | async-done | bytes 589840 | tf_op jit(solution)/shard_map/reduce_scatter | solution.py:271
  710.6 62.2 %all-reduce.16 = (bf16[1536]{0:T(1024)(128)(2,1)}, bf16[768]{0:T(1024)(128)(2,1)}, bf16[768]{0:T(1024)(128)(2,1)}, bf16[768]{0:T(1024)(128)(2,1)}, bf16[768]{0:T...) all-reduce(f32[1536]{0:T(1024)S(1)} %pad_maximum_fusion.2, ...), channel_id=4, replica_groups=mesh['enc'=2,'batch'=16] {'batch'}, use_global_device_ids=true, to_apply=%region_20.21.clone | all-reduce | flops 9216 | bytes 55296
  789.1 58.6 %all-reduce.17 = (bf16[1536]{0:T(1024)(128)(2,1)}, bf16[768]{0:T(1024)(128)(2,1)}, bf16[768]{0:T(1024)(128)(2,1)}, bf16[768]{0:T(1024)(128)(2,1)}, bf16[768]{0:T...) all-reduce(bf16[1536]{0:T(1024)(128)(2,1)S(1)} %dynamic-update-slic, ...), channel_id=1, replica_groups=mesh['enc'=2,'batch'=16] {'batch'}, use_global_device_ids=true, to_apply=%add | all-reduce | flops 9216 | bytes 36864
  857.9 8.0 add_bitcast_fusion
  872.3 5.5 bitcast_convert_fusion.2
  877.8 6.9 bitcast_convert_fusion
  884.6 10.4 %all-gather.9.cloned.1.call-done = bf16[768,3072]{1,0:T(8,128)(2,1)} async-done(((bf16[48,3072]{1,0:T(8,128)(2,1)}), bf16[768,3072]{1,0:T(8,128)(2,1)}) %all-gather.9.cloned.1.call-update) | async-done | bytes 4718608 | tf_op jit(solution)/shard_map/all_gather | solution.py:297
  895.0 7.4 bitcast_convert_fusion.1
  (317 shorter events, 180.8 us)
Async XLA Ops:
  7.2 209.8 %reduce-scatter.8.cloned.1.call-start = ((), (), s32[]{:S(2)}) async-start(), calls=%async_computation.5 | async-start | bytes 835584 | tf_op jit(solution)/shard_map/reduce_scatter | solution.py:199
  77.4 40.4 %slice-start = ((s8[4718592]{0:T(1024)(128)(4,1)}), s8[4194304]{0:T(1024)(128)(4,1)S(1)}, s32[]{:S(2)}) async-start(s8[4718592]{0:T(1024)(128)(4,1)} %bitcast.230), calls=%async_computation.14 | async-start | bytes 8388608
  79.1 38.7 %copy-start.9 = (f32[1024,768]{0,1:T(8,128)}, f32[1024,768]{0,1:T(8,128)S(1)}, u32[]{:S(2)}) copy-start(f32[1024,768]{0,1:T(8,128)S(1)} %get-tuple-element.312) | copy-start | bytes 9437188
  79.2 38.6 %copy-start.34 = (f32[1024]{0:T(1024)}, f32[1024]{0:T(1024)S(1)}, u32[]{:S(2)}) copy-start(f32[1024]{0:T(1024)S(1)} %broadcast_multiply_fusion.1) | copy-start | bytes 12292
  81.8 36.1 %copy-start.45 = (f32[1024]{0:T(1024)}, f32[1024]{0:T(1024)S(1)}, u32[]{:S(2)}) copy-start(f32[1024]{0:T(1024)S(1)} %fusion.85) | copy-start | bytes 12292
  81.8 36.0 %copy-start.41 = (f32[768]{0:T(1024)}, f32[768]{0:T(1024)S(1)}, u32[]{:S(2)}) copy-start(f32[768]{0:T(1024)S(1)} %get-tuple-element.325) | copy-start | bytes 9220
  81.8 36.0 %copy-start.54 = (f32[768]{0:T(1024)}, f32[768]{0:T(1024)S(1)}, u32[]{:S(2)}) copy-start(f32[768]{0:T(1024)S(1)} %get-tuple-element.324) | copy-start | bytes 9220
  81.8 36.0 %copy-start.56 = (f32[768]{0:T(1024)S(1)}, f32[768]{0:T(1024)}, u32[]{:S(2)}) copy-start(f32[768]{0:T(1024)} %convert_reduce_fusion.6) | copy-start | bytes 9220
  81.9 36.0 %slice-start.1 = ((s8[4718592]{0:T(1024)(128)(4,1)}), s8[524288]{0:T(1024)(128)(4,1)S(1)}, s32[]{:S(2)}) async-start(s8[4718592]{0:T(1024)(128)(4,1)} %bitcast.230), calls=%async_computation.15 | async-start | bytes 1048576
  125.6 106.6 %copy-start.23 = (f32[1024]{0:T(1024)}, f32[1024]{0:T(1024)S(1)}, u32[]{:S(2)}) copy-start(f32[1024]{0:T(1024)S(1)} %broadcast_multiply_fusion) | copy-start | bytes 12292
  126.7 105.6 %copy-start.27 = (f32[1024]{0:T(1024)}, f32[1024]{0:T(1024)S(1)}, u32[]{:S(2)}) copy-start(f32[1024]{0:T(1024)S(1)} %fusion.86) | copy-start | bytes 12292
  128.1 6.9 collective-permute-start
  135.0 25.5 %copy-start.61 = (s32[8]{0:T(128)}, s32[8]{0:T(128)S(1)}, u32[]{:S(2)}) copy-start(s32[8]{0:T(128)S(1)} %dynamic_slice.40) | copy-start | bytes 100
  163.0 233.9 %reduce-scatter.10.cloned.1.call-start = ((), (), s32[]{:S(2)}) async-start(), calls=%async_computation.7 | async-start | bytes 2506752 | tf_op jit(solution)/shard_map/reduce_scatter | solution.py:267
  218.4 8.0 collective-permute-start.1
  221.7 4.0 collective-permute-start.2
  235.4 19.3 %copy-start.10 = (f32[1024,768]{0,1:T(8,128)S(1)}, f32[1024,768]{0,1:T(8,128)}, u32[]{:S(2)}) copy-start(f32[1024,768]{0,1:T(8,128)} %copy-done.9) | copy-start | bytes 9437188
  235.4 19.3 %copy-start.35 = (f32[1024]{0:T(1024)S(1)}, f32[1024]{0:T(1024)}, u32[]{:S(2)}) copy-start(f32[1024]{0:T(1024)} %copy-done.34) | copy-start | bytes 12292
  235.4 19.3 %copy-start.42 = (f32[768]{0:T(1024)S(1)}, f32[768]{0:T(1024)}, u32[]{:S(2)}) copy-start(f32[768]{0:T(1024)} %copy-done.41) | copy-start | bytes 9220
  235.4 19.3 %copy-start.46 = (f32[1024]{0:T(1024)S(1)}, f32[1024]{0:T(1024)}, u32[]{:S(2)}) copy-start(f32[1024]{0:T(1024)} %copy-done.45) | copy-start | bytes 12292
  254.6 11.2 %copy-start.38 = (f32[1024]{0:T(1024)S(1)}, f32[1024]{0:T(1024)}, u32[]{:S(2)}) copy-start(f32[1024]{0:T(1024)} %copy-done.37) | copy-start | bytes 12292
  286.9 176.8 %reduce-scatter.16.cloned.1.call-start = ((), (), s32[]{:S(2)}) async-start(), calls=%async_computation.13 | async-start | bytes 7520256 | tf_op jit(solution)/shard_map/reduce_scatter | solution.py:265
  374.9 204.7 %reduce-scatter.14.cloned.1.call-start = ((), (), s32[]{:S(2)}) async-start(), calls=%async_computation.11 | async-start | bytes 10027008 | tf_op jit(solution)/shard_map/reduce_scatter | solution.py:273
  384.9 310.3 %reduce-scatter.12.cloned.1.call-start = ((), (), s32[]{:S(2)}) async-start(), calls=%async_computation.9 | async-start | bytes 10027008 | tf_op jit(solution)/shard_map/reduce_scatter | solution.py:271
  396.8 305.5 %copy-start.24 = (f32[1024]{0:T(1024)S(1)}, f32[1024]{0:T(1024)}, u32[]{:S(2)}) copy-start(f32[1024]{0:T(1024)} %copy-done.23) | copy-start | bytes 12292
  396.8 305.5 %copy-start.28 = (f32[1024]{0:T(1024)S(1)}, f32[1024]{0:T(1024)}, u32[]{:S(2)}) copy-start(f32[1024]{0:T(1024)} %copy-done.27) | copy-start | bytes 12292
  396.8 305.5 %copy-start.31 = (f32[768]{0:T(1024)S(1)}, f32[768]{0:T(1024)}, u32[]{:S(2)}) copy-start(f32[768]{0:T(1024)} %copy-done.29) | copy-start | bytes 9220
  396.8 305.5 %copy-start.33 = (f32[768]{0:T(1024)S(1)}, f32[768]{0:T(1024)}, u32[]{:S(2)}) copy-start(f32[768]{0:T(1024)} %copy-done.32) | copy-start | bytes 9220
  396.9 472.5 %all-gather.7.cloned.1.call-start = ((), (), s32[]{:S(2)}) async-start(), calls=%async_computation.8 | async-start | bytes 1253376 | tf_op jit(solution)/shard_map/all_gather | solution.py:285
  398.5 473.7 %all-gather.5.cloned.1.call-start = ((), (), s32[]{:S(2)}) async-start(), calls=%async_computation.6 | async-start | bytes 3760128 | tf_op jit(solution)/shard_map/all_gather | solution.py:279
  465.4 412.3 %all-gather.11.cloned.1.call-start = ((), (), s32[]{:S(2)}) async-start(), calls=%async_computation.12 | async-start | bytes 5013504 | tf_op jit(solution)/shard_map/all_gather | solution.py:303
  581.4 313.6 %all-gather.9.cloned.1.call-start = ((), (), s32[]{:S(2)}) async-start(), calls=%async_computation.10 | async-start | bytes 5013504 | tf_op jit(solution)/shard_map/all_gather | solution.py:297
  (59 other events, 192.4 us)
Sparse Core Ops, SparseCore 0:
  163.2 53.7 reduce-scatter.7
  287.0 61.3 reduce-scatter.9
  375.0 88.5 reduce-scatter.15
  468.7 110.8 reduce-scatter.13
  584.1 111.0 reduce-scatter.11
  697.7 38.2 all-gather.6
  738.5 45.9 all-gather.4
  787.0 52.8 all-gather.10
  843.0 51.9 all-gather.8
where the time goes:
time: 920 us; the launch traced here: 909 us
  waiting for transfers between devices  358 us (39%)
  matrix products  189 us (21%)
  blocking collectives  143 us (16%)
  local copies, waits for them, and re-layouts  115 us (12%)
  other arithmetic  77.7 us (8%)
  between operations  18.8 us (2%)
    unnamed x2, blocking collectives  121 us
    reduce_scatter x1, waiting for transfers between devices, shards(): lax.psum_scatter(gradient_contraction, 'batch', scatter_dimension=0, tile...  114 us
    reduce_scatter x1, waiting for transfers between devices, shards(): lax.psum_scatter(gradient_expansion, 'batch', scatter_dimension=0, tiled=...  114 us
    reduce_scatter x1, waiting for transfers between devices, shards(): lax.psum_scatter(gradient_projection, 'batch', scatter_dimension=0, tiled...  65.1 us
    reduce_scatter x1, waiting for transfers between devices, shards(): lax.psum_scatter(jnp.einsum('qs,qd->sd', logits_gradient, local_questions...  53.9 us
    unnamed x154, local copies, waits for them, and re-layouts  51.2 us
    dot_general x1, matrix products, shards(): jnp.dot(first_low, expand_matrix, preferred_element_type=FLOAT_KIND)  35.9 us
    all_gather x1, blocking collectives, shards(): lax.all_gather(passage_embedding, 'batch', axis=0, tiled=True)  22.7 us
  transfers between devices with their start and end apart: 12, of which 6 were waited for; matrix products, arithmetic and copies ran while one was open for 20% of the time, Pallas kernels for 0%

commit v1 on v0

--- a/solution.py
+++ b/solution.py
@@ -101,6 +101,49 @@
         jnp.arange(score_matrix.shape[1], dtype=jnp.int32)[None, :] == target_row_list[:, None]
     )
     return to_low(LOSS_WEIGHT * (probability - target_hit.astype(FLOAT_KIND)))
+
+
+def bit_count(axis):
+    return lax.axis_size(axis).bit_length() - 1
+
+
+def split_by_bit(value, bit):
+    half = value.shape[0] // 2
+    keep = lax.dynamic_slice_in_dim(value, bit * half, half, 0)
+    send = lax.dynamic_slice_in_dim(value, (1 - bit) * half, half, 0)
+    return keep, send
+
+
+def joined_by_bit(mine, other, bit):
+    low_part = jnp.where(bit == 0, mine, other)
+    high_part = jnp.where(bit == 0, other, mine)
+    return jnp.concatenate([low_part, high_part], axis=0)
+
+
+def scatter_sum(value, axis):
+    index = lax.axis_index(axis)
+    for apart in range(bit_count(axis)):
+        keep, send = split_by_bit(value, (index >> apart) & 1)
+        arrived = swapped(send, axis, apart)
+        value = to_low(keep.astype(FLOAT_KIND) + arrived.astype(FLOAT_KIND))
+    return value
+
+
+def gather_all(value, axis):
+    index = lax.axis_index(axis)
+    for apart in reversed(range(bit_count(axis))):
+        value = joined_by_bit(value, swapped(value, axis, apart), (index >> apart) & 1)
+    return value
+
+
+def total_sum(value, axis):
+    for apart in range(bit_count(axis)):
+        value = value + swapped(value, axis, apart)
+    return value
+
+
+def weight_total(value):
+    return gather_all(scatter_sum(to_low(value), "batch"), "batch").astype(FLOAT_KIND)
 
 
 def shards(
@@ -172,45 +215,45 @@
     encoded, second_back = jax.vjp(layer_norm, normed_one + shrunk, rescale_row, recenter_row)
     encoded_low = to_low(encoded)
     slot_count = passage_starts.shape[0]
-    half_count = slot_count // 2
     slot_index = jnp.arange(slot_count, dtype=jnp.int32)
     summary_rows = jnp.where(is_passage, passage_starts, slot_index * QLEN)
     picker = summary_rows[:, None] == position[None, :]
     summary_local = to_low(
         jnp.dot(picker.astype(BRAIN), encoded_low, preferred_element_type=FLOAT_KIND)
     )
-    partner = swapped(summary_local, "enc", 0)
-    passage_embedding = jnp.where(is_passage, summary_local, partner)
-    question_embedding = jnp.where(is_passage, partner, summary_local)
     smoothing_divisor = SHARPNESS_DIVISOR / math.sqrt(feature_breadth)
+    lane = jnp.arange(128, dtype=jnp.int32)[None, :]
+    target_column = positives[:, None]
+    digits = jnp.where(lane == 0, target_column // 128, jnp.where(lane == 1, target_column % 128, 0))
+    parcel = jnp.concatenate([summary_local, digits.astype(BRAIN)], axis=1)
+    both = joined_by_bit(parcel[None], swapped(parcel, "enc", 0)[None], enc_index)
+    index = lax.axis_index("batch")
+    for apart in range(bit_count("batch")):
+        mine_bit = (index >> apart) & 1
+        other = swapped(both, "batch", apart)
+        both = jnp.concatenate(
+            [jnp.where(mine_bit == 0, both, other), jnp.where(mine_bit == 0, other, both)], axis=1
+        )
+    question_all = both[0, :, :feature_breadth]
+    passage_all = both[1, :, :feature_breadth]
+    digits_all = both[0, :, feature_breadth : feature_breadth + 2].astype(jnp.int32)
+    target_all = digits_all[:, 0] * 128 + digits_all[:, 1]
     valid_entries = (slot_index[None, :] < passage_counts[:, None]).reshape(-1)
-    collected_rows = lax.all_gather(passage_embedding, "batch", axis=0, tiled=True)
-    local_questions = lax.dynamic_slice_in_dim(
-        question_embedding, enc_index * half_count, half_count, 0
-    )
-    local_targets = lax.dynamic_slice_in_dim(positives, enc_index * half_count, half_count, 0)
     logits_gradient = logit_gradients(
-        local_questions, local_targets, collected_rows, valid_entries, smoothing_divisor
-    )
-    gradient_questions = (
-        jnp.dot(logits_gradient, collected_rows, preferred_element_type=FLOAT_KIND)
+        question_all, target_all, passage_all, valid_entries, smoothing_divisor
+    )
+    own_rows = jnp.where(
+        is_passage,
+        lax.dynamic_slice_in_dim(logits_gradient, index * slot_count, slot_count, 1).T,
+        lax.dynamic_slice_in_dim(logits_gradient, index * slot_count, slot_count, 0),
+    )
+    gradient_summary = (
+        jnp.dot(
+            own_rows,
+            jnp.where(is_passage, question_all, passage_all),
+            preferred_element_type=FLOAT_KIND,
+        )
         * smoothing_divisor
-    )
-    gradient_passages = lax.psum_scatter(
-        jnp.einsum("qs,qd->sd", logits_gradient, local_questions, preferred_element_type=FLOAT_KIND)
-        * smoothing_divisor,
-        "batch",
-        scatter_dimension=0,
-        tiled=True,
-    )
-    back_questions, back_passages = (
-        swapped(gradient_questions.astype(jnp.bfloat16), "enc", 0).astype(gradient_questions.dtype),
-        swapped(gradient_passages.astype(jnp.bfloat16), "enc", 0).astype(gradient_passages.dtype),
-    )
-    gradient_summary = jnp.where(
-        is_passage,
-        gradient_passages + back_passages,
-        jnp.concatenate([gradient_questions, back_questions], axis=0),
     )
     gradient_encoded = cotangent[0].astype(FLOAT_KIND) + jnp.einsum(
         "ct,cd->td", picker.astype(FLOAT_KIND), gradient_summary, precision=lax.Precision.HIGHEST
@@ -261,60 +304,28 @@
     tokens_gradient = gradient_one + jnp.einsum(
         "te,de->td", gradient_packed, focus_weighting_array, preferred_element_type=FLOAT_KIND
     )
-    every_share = (
-        lax.psum_scatter(gradient_projection, "batch", scatter_dimension=0, tiled=True),
-        lax.psum_scatter(gradient_offsets, "batch", scatter_dimension=0, tiled=True),
-        lax.psum_scatter(gradient_merger, "batch", scatter_dimension=0, tiled=True),
-        lax.psum_scatter(gradient_adjust, "batch", scatter_dimension=0, tiled=True),
-        lax.psum_scatter(gradient_scaling, "batch", scatter_dimension=0, tiled=True),
-        lax.psum_scatter(gradient_centering, "batch", scatter_dimension=0, tiled=True),
-        lax.psum_scatter(gradient_expansion, "batch", scatter_dimension=0, tiled=True),
-        lax.psum_scatter(gradient_lifting, "batch", scatter_dimension=0, tiled=True),
-        lax.psum_scatter(gradient_contraction, "batch", scatter_dimension=0, tiled=True),
-        lax.psum_scatter(gradient_settling, "batch", scatter_dimension=0, tiled=True),
-        lax.psum_scatter(gradient_rescale, "batch", scatter_dimension=0, tiled=True),
-        lax.psum_scatter(gradient_recenter, "batch", scatter_dimension=0, tiled=True),
-    )
-    overall_aggregate = (
-        lax.all_gather(every_share[0].astype(jnp.bfloat16), "batch", axis=0, tiled=True).astype(
-            jnp.float32
-        ),
-        lax.all_gather(every_share[1].astype(jnp.bfloat16), "batch", axis=0, tiled=True).astype(
-            jnp.float32
-        ),
-        lax.all_gather(every_share[2].astype(jnp.bfloat16), "batch", axis=0, tiled=True).astype(
-            jnp.float32
-        ),
-        lax.all_gather(every_share[3].astype(jnp.bfloat16), "batch", axis=0, tiled=True).astype(
-            jnp.float32
-        ),
-        lax.all_gather(every_share[4].astype(jnp.bfloat16), "batch", axis=0, tiled=True).astype(
-            jnp.float32
-        ),
-        lax.all_gather(every_share[5].astype(jnp.bfloat16), "batch", axis=0, tiled=True).astype(
-            jnp.float32
-        ),
-        lax.all_gather(every_share[6].astype(jnp.bfloat16), "batch", axis=0, tiled=True).astype(
-            jnp.float32
-        ),
-        lax.all_gather(every_share[7].astype(jnp.bfloat16), "batch", axis=0, tiled=True).astype(
-            jnp.float32
-        ),
-        lax.all_gather(every_share[8].astype(jnp.bfloat16), "batch", axis=0, tiled=True).astype(
-            jnp.float32
-        ),
-        lax.all_gather(every_share[9].astype(jnp.bfloat16), "batch", axis=0, tiled=True).astype(
-            jnp.float32
-        ),
-        lax.all_gather(every_share[10].astype(jnp.bfloat16), "batch", axis=0, tiled=True).astype(
-            jnp.float32
-        ),
-        lax.all_gather(every_share[11].astype(jnp.bfloat16), "batch", axis=0, tiled=True).astype(
-            jnp.float32
-        ),
-    )
-    attend_total = overall_aggregate[:6]
-    expand_total = overall_aggregate[6:]
+    small = (
+        gradient_offsets,
+        gradient_adjust,
+        gradient_scaling,
+        gradient_centering,
+        gradient_lifting,
+        gradient_settling,
+        gradient_rescale,
+        gradient_recenter,
+    )
+    small_total = total_sum(jnp.concatenate(small), "batch")
+    small_parts = []
+    place = 0
+    for part in small:
+        small_parts.append(small_total[place : place + part.shape[0]])
+        place += part.shape[0]
+    total_contraction = weight_total(gradient_contraction)
+    total_expansion = weight_total(gradient_expansion)
+    total_merger = weight_total(gradient_merger)
+    total_projection = weight_total(gradient_projection)
+    attend_total = (total_projection, small_parts[0], total_merger, *small_parts[1:4])
+    expand_total = (total_expansion, small_parts[4], total_contraction, *small_parts[5:8])
     return (
         to_low(encoded)[None],
         tokens_gradient[None],

time: 920 us -> 631 us (0.69)
  waiting for transfers between devices: 358 us -> 209 us
  blocking collectives: 143 us -> 0 us
  starting transfers between devices: 6.67 us -> 42.6 us
  matrix products: 189 us -> 172 us
  between operations: 18.8 us -> 2.55 us
  other arithmetic: 77.7 us -> 88.8 us
    reduce_scatter x5 -> x0, waiting for transfers between devices: 347 us -> none  [the longest x1 114 us: shards(): lax.psum_scatter(gradient_contraction, 'batch', scatter_dimension=0, tile...]
    ppermute x3 -> x41, waiting for transfers between devices: 0.71 us -> 209 us  [swapped(): return lax.ppermute(value, axis, pairs)]
    unnamed x2 -> x0, blocking collectives: 121 us -> none
    ppermute x3 -> x41, starting transfers between devices: 6.3 us -> 42.6 us  [swapped(): return lax.ppermute(value, axis, pairs)]
    broadcast_in_dim x5 -> x0, other arithmetic: 23.9 us -> none  [the longest x1 7.37 us: shards(): expand_total[0][None]]
    all_gather x1 -> x0, blocking collectives: 22.7 us -> none  [shards(): lax.all_gather(passage_embedding, 'batch', axis=0, tiled=True)]
    unnamed x154 -> x175, local copies, waits for them, and re-layouts: 51.2 us -> 39.6 us
    convert_element_type x2 -> x19, other arithmetic: 14.4 us -> 25.7 us  [to_low(): return values.astype(BRAIN)]
  transfers between devices with their start and end apart: 12 -> 41, of which waited for: 6 -> 23; matrix products, arithmetic and copies ran while one was open for 20% -> 25% of each run, Pallas kernels for 0% -> 0%
where the time goes in v1:
time: 631 us; the launch traced here: 621 us
  waiting for transfers between devices  209 us (33%)
  matrix products  172 us (27%)
  local copies, waits for them, and re-layouts  106 us (17%)
  other arithmetic  88.8 us (14%)
  starting transfers between devices  42.6 us (7%)
    ppermute x41, waiting for transfers between devices, swapped(): return lax.ppermute(value, axis, pairs)  209 us
    ppermute x41, starting transfers between devices, swapped(): return lax.ppermute(value, axis, pairs)  42.6 us
    unnamed x175, local copies, waits for them, and re-layouts  39.6 us
    dot_general x1, matrix products, shards(): jnp.dot(first_low, expand_matrix, preferred_element_type=FLOAT_KIND)  35.9 us
    convert_element_type x19, other arithmetic, to_low(): return values.astype(BRAIN)  25.7 us
    dot_general x1, matrix products, shards(): jnp.einsum('td,fd->tf', gradient_shrunk, shrink_matrix, preferred_element...  19.3 us
    convert_element_type x4, other arithmetic, weight_total(): gather_all(scatter_sum(to_low(value), 'batch'), 'batch').astype(FLOAT_KIND)  14.5 us
    dot_general x4, matrix products, block_scores(): jnp.einsum('qhd,khd->hqk', queries, key_rows, preferred_element_type=FLOA...  13.7 us
  transfers between devices with their start and end apart: 41, of which 23 were waited for; matrix products, arithmetic and copies ran while one was open for 25% of the time, Pallas kernels for 0%

profile of v1, /device:TPU:0, one launch (start us, length us, event | category | flops | bytes accessed | tf_op | source)
XLA Modules:
  0.0 621.0 jit_solution(8531742376983858688)
XLA Ops:
  9.8 7.3 %add_convert_fusion.1 = bf16[1024,2304]{1,0:T(8,128)(2,1)} fusion(f32[2304]{0:T(1024)S(1)} %pad_maximum_fusion.19, bf16[1,768,2304]{2,1,0:T(8,128)(2,1)S(1)} %copy-done, bf16[1,1024,768]{2,1,0:T(8,128)(2,1)} %param.22), kind=kOutput, calls=%fused_computation.78 | convolution fusion | flops 3628597248 | bytes 9839616 | tf_op jit(solution)/shard_map/dot_general | solution.py:199
  17.1 6.6 %copy.53 = bf16[1024,2304]{0,1:T(8,128)(2,1)} copy(bf16[1024,2304]{1,0:T(8,128)(2,1)} %add_convert_fusion.1) | data formatting | bytes 9437184 | tf_op jit(solution)/shard_map/convert_element_type | solution.py:37
  23.7 8.8 %reshape.391 = bf16[2,512,3,12,64]{1,0,4,3,2:T(2,128)(2,1)} reshape(bf16[1024,2304]{0,1:T(8,128)(2,1)} %copy.53) | data formatting | bytes 9437184 | tf_op jit(solution)/shard_map/reshape | solution.py:201
  42.3 26.5 %while.26 = (s32[]{:T(128)}, bf16[2,512,12,64]{1,3,2,0:T(8,128)(2,1)}, f32[2,12,512,1]{2,1,3,0:T(8,128)}, bf16[2,512,12,64]{1,3,2,0:T(8,128)(2,1)}, s32[2,512]{1...) while((s32[]{:T(128)}, ...), condition=%wide.region_3.4_spmd, body=%wide.region_0.3_spmd.sunk | while | flops 840558592 | bytes 43204736 | solution.py:205
  76.9 35.9 %multiply_convert_fusion.1 = (bf16[1024,3072]{1,0:T(8,128)(2,1)}, f32[1024,3072]{1,0:T(8,128)}, f32[1024,3072]{1,0:T(8,128)}) fusion(f32[3072]{0:T(1024)S(1)} %bitcast.263, bf16[1,768,3072]{2,1,0:T(8,128)(2,1)S(1)} %bitcast.269, f32[1024,768]{0,1:T(8,128)S(1)} %get-tuple-element.282, f32[768]{0:T(1024)S(1)} %get-tuple-element.292, ...), kind=kOutput, calls=%fused_computation.63 | convolution fusion | flops 5043388416 | bytes 39348224 | tf_op jit(solution)/shard_map/dot_general | solution.py:212
  112.9 7.9 %fusion.107 = (f32[1024]{0:T(1024)S(1)}, f32[1024,768]{0,1:T(8,128)S(1)}) fusion(f32[768]{0:T(1024)S(1)} %copy-done.63, bf16[1024,3072]{1,0:T(8,128)(2,1)} %get-tuple-element.220, bf16[1,3072,768]{2,1,0:T(8,128)(2,1)S(1)} %bitcast.267, f32[768]{0:T(1024)S(1)} %get-tuple-element.292, f32[768]{0:T(1024)S(1)} %get-tuple-element.293, f32[1024]{0:T(1024)S(1)} %fusion.93, ...), kind=kOutput, calls=%fused_computation.304 | convolution fusion | flops 4837342208 | bytes 17323008 | tf_op jit(solution)/shard_map/dot_general | solution.py:214
  167.0 8.0 %collective-permute-done.4 = bf16[2,128,896]{2,1,0:T(8,128)(2,1)} collective-permute-done((bf16[2,128,896]{2,1,0:T(8,128)(2,1)}, bf16[2,128,896]{2,1,0:T(8,128)(2,1)}, u32[]{:S(2)}, u32[]{:S(2)}) %collective-permute-start.4) | collective-permute-done | bytes 458784 | tf_op jit(solution)/shard_map/ppermute | solution.py:23
  182.5 5.7 multiply_reduce_fusion.1
  192.8 6.9 %convolution_convert_fusion = bf16[3072,768]{1,0:T(8,128)(2,1)} fusion(bf16[1024,3072]{1,0:T(8,128)(2,1)S(1)} %bitcast.271, bf16[1024,768]{0,1:T(8,128)(2,1)S(1)} %get-tuple-element.211), kind=kOutput, calls=%fused_computation.79 | convolution fusion | flops 4834197504 | bytes 12582912 | tf_op jit(solution)/shard_map/tf,td->fd/dot_general | solution.py:264
  199.8 19.3 %convert_reduce_fusion = (f32[3072]{0:T(1024)}, bf16[1024,3072]{1,0:T(8,128)(2,1)}) fusion(f32[1024,3072]{1,0:T(8,128)} %get-tuple-element.221, bf16[1024,768]{0,1:T(8,128)(2,1)} %copy-done.25, bf16[1,3072,768]{2,1,0:T(8,128)(2,1)} %param.32, f32[1024,3072]{1,0:T(8,128)} %get-tuple-element.283, f32[3072]{0:T(1024)S(1)} %bitcast.264), kind=kOutput, calls=%fused_computation.61 | convolution fusion | flops 4885312512 | bytes 37773312 | tf_op jit(solution)/shard_map/td,fd->tf/dot_general | solution.py:267
  219.1 10.9 %multiply_reduce_fusion.2 = (f32[768]{0:T(1024)}, f32[1024]{0:T(1024)S(1)}, f32[768]{0:T(1024)}, f32[1024,768]{0,1:T(8,128)S(1)}) fusion(f32[1024,768]{0,1:T(8,128)S(1)} %copy-done.9, f32[1024]{0:T(1024)S(1)} %copy-done.54, f32[1024]{0:T(1024)S(1)} %copy-done.44, f32[768]{0:T(1024)S(1)} %copy-done.52, bf16[1024,3072]{1,0:T(8,128)(2,1)} %get-tuple-element.291, ...), kind=kOutput, calls=%fused_computation.105 | convolution fusion | flops 4839699456 | bytes 20472832 | tf_op jit(solution)/shard_map/tf,df->td/dot_general | solution.py:276
  230.0 7.5 %convolution_convert_fusion.1 = bf16[768,3072]{1,0:T(8,128)(2,1)} fusion(bf16[1024,3072]{1,0:T(8,128)(2,1)S(1)} %copy-done.76, f32[1024,768]{0,1:T(8,128)S(1)} %copy-done.9, f32[768]{0:T(1024)S(1)} %copy-done.62, f32[768]{0:T(1024)S(1)} %copy-done.52, f32[1024]{0:T(1024)S(1)} %copy-done.54, f32[1024]{0:T(1024)S(1)} %copy-done.44), kind=kOutput, calls=%fused_computation.80 | convolution fusion | flops 4838129664 | bytes 14170112 | tf_op jit(solution)/shard_map/td,tf->df/dot_general | solution.py:273
  255.1 53.3 %while.27 = (s32[]{:T(128)}, bf16[2,512,12,64]{1,3,2,0:T(8,128)(2,1)}, bf16[2,512,12,64]{1,3,2,0:T(8,128)(2,1)}, bf16[2,512,12,64]{1,3,2,0:T(8,128)(2,1)}, bf16[...) while((s32[]{:T(128)}, ...), condition=%wide.region_16.17_spmd, body=%wide.region_14.16_spmd.sunk | while | flops 2061494272 | bytes 156175728 | solution.py:289
  263.4 6.8 %multiply_reduce_fusion.8 = (f32[12,512]{1,0:T(8,128)S(1)}, f32[12,512,512]{1,2,0:T(8,128)}) fusion(f32[12,512,512]{1,2,0:T(8,128)S(1)} %fusion.149, f32[12,512]{1,0:T(8,128)S(1)} %dynamic-slice_bitcast_fusion.3, pred[512,512]{0,1:T(8,128)(4,1)S(1)} %broadcast_compare_fusion.5, bf16[2,512,12,64]{1,3,2,0:T(8,128)(2,1)S(1)} %copy-done.6, ...), kind=kOutput, calls=%fused_computation.25.clone.1 | convolution fusion | flops 418375680 | bytes 27059200 | tf_op jit(solution)/shard_map/while/body/eval_jaxpr/qhd,khd->hqk/dot_general | solution.py:67
  270.2 7.1 %multiply_convert_fusion.4 = bf16[12,512,512]{1,2,0:T(8,128)(2,1)S(1)} fusion(f32[12,512,512]{1,2,0:T(8,128)} %get-tuple-element.412, f32[12,512,512]{1,2,0:T(8,128)S(1)} %fusion.149, f32[12,512]{1,0:T(8,128)S(1)} %get-tuple-element.413, f32[12,512]{1,0:T(8,128)S(1)} %dynamic-slice_bitcast_fusion.3, pred[512,512]{0,1:T(8,128)(4,1)S(1)} %broadcast_compare_fusion.5), kind=kLoop, calls=%fused_computation.24.clone.1 | loop fusion | flops 18874368 | bytes 31768576 | tf_op jit(solution)/shard_map/while/body/eval_jaxpr/convert_element_type | solution.py:37
  290.1 6.8 %multiply_reduce_fusion.8 = (f32[12,512]{1,0:T(8,128)S(1)}, f32[12,512,512]{1,2,0:T(8,128)}) fusion(f32[12,512,512]{1,2,0:T(8,128)S(1)} %fusion.149, f32[12,512]{1,0:T(8,128)S(1)} %dynamic-slice_bitcast_fusion.3, pred[512,512]{0,1:T(8,128)(4,1)S(1)} %broadcast_compare_fusion.5, bf16[2,512,12,64]{1,3,2,0:T(8,128)(2,1)S(1)} %copy-done.6, ...), kind=kOutput, calls=%fused_computation.25.clone.1 | convolution fusion | flops 418375680 | bytes 27059200 | tf_op jit(solution)/shard_map/while/body/eval_jaxpr/qhd,khd->hqk/dot_general | solution.py:67
  296.9 7.1 %multiply_convert_fusion.4 = bf16[12,512,512]{1,2,0:T(8,128)(2,1)S(1)} fusion(f32[12,512,512]{1,2,0:T(8,128)} %get-tuple-element.412, f32[12,512,512]{1,2,0:T(8,128)S(1)} %fusion.149, f32[12,512]{1,0:T(8,128)S(1)} %get-tuple-element.413, f32[12,512]{1,0:T(8,128)S(1)} %dynamic-slice_bitcast_fusion.3, pred[512,512]{0,1:T(8,128)(4,1)S(1)} %broadcast_compare_fusion.5), kind=kLoop, calls=%fused_computation.24.clone.1 | loop fusion | flops 18874368 | bytes 31768576 | tf_op jit(solution)/shard_map/while/body/eval_jaxpr/convert_element_type | solution.py:37
  334.9 9.4 %copy.67 = bf16[2,512,3,12,64]{1,0,4,3,2:T(2,128)(2,1)} copy(bf16[2,512,3,12,64]{1,4,3,0,2:T(8,128)(2,1)} %get-tuple-element.215) | data formatting | bytes 9437184 | tf_op jit(solution)/shard_map/stack | solution.py:293
  397.9 6.6 %collective-permute-done.6 = bf16[192,2304]{1,0:T(8,128)(2,1)} collective-permute-done((bf16[192,2304]{1,0:T(8,128)(2,1)}, bf16[192,2304]{1,0:T(8,128)(2,1)}, u32[]{:S(2)}, u32[]{:S(2)}) %collective-permute-start.6) | collective-permute-done | bytes 884768 | tf_op jit(solution)/shard_map/ppermute | solution.py:23
  409.9 7.8 %collective-permute-done.7 = bf16[96,2304]{1,0:T(8,128)(2,1)S(1)} collective-permute-done((bf16[96,2304]{1,0:T(8,128)(2,1)S(1)}, bf16[96,2304]{1,0:T(8,128)(2,1)S(1)}, u32[]{:S(2)}, u32[]{:S(2)}) %collective-permute-start.7) | collective-permute-done | bytes 442400 | tf_op jit(solution)/shard_map/ppermute | solution.py:23
  419.7 9.7 %collective-permute-done.8 = bf16[48,2304]{1,0:T(8,128)(2,1)S(1)} collective-permute-done((bf16[48,2304]{1,0:T(8,128)(2,1)S(1)}, bf16[48,2304]{1,0:T(8,128)(2,1)S(1)}, u32[]{:S(2)}, u32[]{:S(2)}) %collective-permute-start.8) | collective-permute-done | bytes 221216 | tf_op jit(solution)/shard_map/ppermute | solution.py:23
  433.4 6.3 %collective-permute-done.9 = bf16[48,2304]{1,0:T(8,128)(2,1)S(1)} collective-permute-done((bf16[48,2304]{1,0:T(8,128)(2,1)S(1)}, bf16[48,2304]{1,0:T(8,128)(2,1)S(1)}, u32[]{:S(2)}, u32[]{:S(2)}) %collective-permute-start.9) | collective-permute-done | bytes 221216 | tf_op jit(solution)/shard_map/ppermute | solution.py:23
  439.8 7.3 %collective-permute-done.26 = bf16[192,3072]{1,0:T(8,128)(2,1)S(1)} collective-permute-done((bf16[192,3072]{1,0:T(8,128)(2,1)S(1)}, bf16[192,3072]{1,0:T(8,128)(2,1)S(1)}, u32[]{:S(2)}, u32[]{:S(2)}) %collective-permute-start.26) | collective-permute-done | bytes 1179680 | tf_op jit(solution)/shard_map/ppermute | solution.py:23
  449.7 20.2 %collective-permute-done.34 = bf16[768,768]{1,0:T(8,128)(2,1)S(1)} collective-permute-done((bf16[768,768]{1,0:T(8,128)(2,1)S(1)}, bf16[768,768]{1,0:T(8,128)(2,1)S(1)}, u32[]{:S(2)}, u32[]{:S(2)}) %collective-permute-start.34) | collective-permute-done | bytes 1179680 | tf_op jit(solution)/shard_map/ppermute | solution.py:23
  473.5 16.1 %collective-permute-done.35 = bf16[384,768]{1,0:T(8,128)(2,1)S(1)} collective-permute-done((bf16[384,768]{1,0:T(8,128)(2,1)S(1)}, bf16[384,768]{1,0:T(8,128)(2,1)S(1)}, u32[]{:S(2)}, u32[]{:S(2)}) %collective-permute-start.35) | collective-permute-done | bytes 589856 | tf_op jit(solution)/shard_map/ppermute | solution.py:23
  490.2 13.8 %collective-permute-done.36 = bf16[192,768]{1,0:T(8,128)(2,1)S(1)} collective-permute-done((bf16[192,768]{1,0:T(8,128)(2,1)S(1)}, bf16[192,768]{1,0:T(8,128)(2,1)S(1)}, u32[]{:S(2)}, u32[]{:S(2)}) %collective-permute-start.36) | collective-permute-done | bytes 294944 | tf_op jit(solution)/shard_map/ppermute | solution.py:23
  507.3 17.8 %collective-permute-done.37 = bf16[192,768]{1,0:T(8,128)(2,1)S(1)} collective-permute-done((bf16[192,768]{1,0:T(8,128)(2,1)S(1)}, bf16[192,768]{1,0:T(8,128)(2,1)S(1)}, u32[]{:S(2)}, u32[]{:S(2)}) %collective-permute-start.37) | collective-permute-done | bytes 294944 | tf_op jit(solution)/shard_map/ppermute | solution.py:23
  525.3 6.1 collective-permute-done.29
  533.3 10.8 %collective-permute-done.38 = bf16[384,768]{1,0:T(8,128)(2,1)S(1)} collective-permute-done((bf16[384,768]{1,0:T(8,128)(2,1)S(1)}, bf16[384,768]{1,0:T(8,128)(2,1)S(1)}, u32[]{:S(2)}, u32[]{:S(2)}) %collective-permute-start.38) | collective-permute-done | bytes 589856 | tf_op jit(solution)/shard_map/ppermute | solution.py:23
  546.0 10.6 %collective-permute-done.30 = bf16[96,3072]{1,0:T(8,128)(2,1)S(1)} collective-permute-done((bf16[96,3072]{1,0:T(8,128)(2,1)S(1)}, bf16[96,3072]{1,0:T(8,128)(2,1)S(1)}, u32[]{:S(2)}, u32[]{:S(2)}) %collective-permute-start.30) | collective-permute-done | bytes 589856 | tf_op jit(solution)/shard_map/ppermute | solution.py:23
  559.0 20.5 %collective-permute-done.39 = bf16[768,768]{1,0:T(8,128)(2,1)S(1)} collective-permute-done((bf16[768,768]{1,0:T(8,128)(2,1)S(1)}, bf16[768,768]{1,0:T(8,128)(2,1)S(1)}, u32[]{:S(2)}, u32[]{:S(2)}) %collective-permute-start.39) | collective-permute-done | bytes 1179680 | tf_op jit(solution)/shard_map/ppermute | solution.py:23
  580.2 23.6 %collective-permute-done.31 = bf16[192,3072]{1,0:T(8,128)(2,1)S(1)} collective-permute-done((bf16[192,3072]{1,0:T(8,128)(2,1)S(1)}, bf16[192,3072]{1,0:T(8,128)(2,1)S(1)}, u32[]{:S(2)}, u32[]{:S(2)}) %collective-permute-start.31) | collective-permute-done | bytes 1179680 | tf_op jit(solution)/shard_map/ppermute | solution.py:23
  (463 shorter events, 278.4 us)
Async XLA Ops:
  153.1 21.9 %collective-permute-start.4 = (bf16[2,128,896]{2,1,0:T(8,128)(2,1)}, bf16[2,128,896]{2,1,0:T(8,128)(2,1)}, u32[]{:S(2)}, u32[]{:S(2)}) collective-permute-start(bf16[2,128,896]{2,1,0:T(8,128)(2,1)} %pad_maximum_fusion.10), channel_id=1, source_target_pairs={{0,8},{1,9},{2,10},{3,11},{4,12},{5,13},{6,14},{7,15},{8,0},{9,1},... | collective-permute-start | bytes 1376264 | tf_op jit(solution)/shard_map/ppermute | solution.py:23
  245.8 73.5 %collective-permute-start.17 = (bf16[384,768]{1,0:T(8,128)(2,1)}, bf16[384,768]{1,0:T(8,128)(2,1)}, u32[]{:S(2)}, u32[]{:S(2)}) collective-permute-start(bf16[384,768]{1,0:T(8,128)(2,1)} %constant_dynamic-slice_fusion.13), channel_id=1, source_target_pairs={{0,1},{1,0},{2,3},{3,2},{4,5},{5,4},{6,7},{7,6},{8,9},{9,8},{10,11... | collective-permute-start | bytes 1769480 | tf_op jit(solution)/shard_map/ppermute | solution.py:23
  320.7 9.5 %collective-permute-start.18 = (bf16[192,768]{1,0:T(8,128)(2,1)S(1)}, bf16[192,768]{1,0:T(8,128)(2,1)S(1)}, u32[]{:S(2)}, u32[]{:S(2)}) collective-permute-start(bf16[192,768]{1,0:T(8,128)(2,1)S(1)} %constant_dynamic-slice_fusion.12), channel_id=1, source_target_pairs={{0,2},{1,3},{2,0},{3,1},{4,6},{5,7},{6,4},{7,5},{8,10},{9,11},{10,... | collective-permute-start | bytes 884744 | tf_op jit(solution)/shard_map/ppermute | solution.py:23
  331.7 16.7 %collective-permute-start.19 = (bf16[96,768]{1,0:T(8,128)(2,1)}, bf16[96,768]{1,0:T(8,128)(2,1)}, u32[]{:S(2)}, u32[]{:S(2)}) collective-permute-start(bf16[96,768]{1,0:T(8,128)(2,1)} %constant_dynamic-slice_fusion.11), channel_id=1, source_target_pairs={{0,4},{1,5},{2,6},{3,7},{4,0},{5,1},{6,2},{7,3},{8,12},{9,13},{10,... | collective-permute-start | bytes 442376 | tf_op jit(solution)/shard_map/ppermute | solution.py:23
  334.9 23.9 %collective-permute-start.13 = (f32[9216]{0:T(1024)}, f32[9216]{0:T(1024)}, u32[]{:S(2)}, u32[]{:S(2)}) collective-permute-start(f32[9216]{0:T(1024)} %constant_dynamic-update-slice_fusion), channel_id=1, source_target_pairs={{0,1},{1,0},{2,3},{3,2},{4,5},{5,4},{6,7},{7,6},{8,9},{9,8},{10,11... | collective-permute-start | bytes 110600 | tf_op jit(solution)/shard_map/ppermute | solution.py:23
  358.7 22.1 %collective-permute-start.5 = (bf16[384,2304]{1,0:T(8,128)(2,1)S(1)}, bf16[384,2304]{1,0:T(8,128)(2,1)S(1)}, u32[]{:S(2)}, u32[]{:S(2)}) collective-permute-start(bf16[384,2304]{1,0:T(8,128)(2,1)S(1)} %dynamic-slice_bitcast_fusion.1), channel_id=1, source_target_pairs={{0,1},{1,0},{2,3},{3,2},{4,5},{5,4},{6,7},{7,6},{8,9},{9,8},{10,11... | collective-permute-start | bytes 5308424 | tf_op jit(solution)/shard_map/ppermute | solution.py:23
  359.6 9.5 %collective-permute-start.14 = (f32[9216]{0:T(1024)S(1)}, f32[9216]{0:T(1024)S(1)}, u32[]{:S(2)}, u32[]{:S(2)}) collective-permute-start(f32[9216]{0:T(1024)S(1)} %add.327), channel_id=1, source_target_pairs={{0,2},{1,3},{2,0},{3,1},{4,6},{5,7},{6,4},{7,5},{8,10},{9,11},{10,... | collective-permute-start | bytes 110600 | tf_op jit(solution)/shard_map/ppermute | solution.py:23
  374.4 32.0 %collective-permute-start.25 = (bf16[384,3072]{1,0:T(8,128)(2,1)}, bf16[384,3072]{1,0:T(8,128)(2,1)}, u32[]{:S(2)}, u32[]{:S(2)}) collective-permute-start(bf16[384,3072]{1,0:T(8,128)(2,1)} %constant_dynamic-slice_fusion.9), channel_id=1, source_target_pairs={{0,1},{1,0},{2,3},{3,2},{4,5},{5,4},{6,7},{7,6},{8,9},{9,8},{10,11... | collective-permute-start | bytes 7077896 | tf_op jit(solution)/shard_map/ppermute | solution.py:23
  375.0 14.3 %collective-permute-start.16 = (f32[9216]{0:T(1024)}, f32[9216]{0:T(1024)}, u32[]{:S(2)}, u32[]{:S(2)}) collective-permute-start(f32[9216]{0:T(1024)} %add.329), channel_id=1, source_target_pairs={{0,8},{1,9},{2,10},{3,11},{4,12},{5,13},{6,14},{7,15},{8,0},{9,1},... | collective-permute-start | bytes 110600 | tf_op jit(solution)/shard_map/ppermute | solution.py:23
  380.7 14.3 %collective-permute-start.24 = (bf16[384,768]{1,0:T(8,128)(2,1)}, bf16[384,768]{1,0:T(8,128)(2,1)}, u32[]{:S(2)}, u32[]{:S(2)}) collective-permute-start(bf16[384,768]{1,0:T(8,128)(2,1)} %pad_maximum_fusion.7), channel_id=1, source_target_pairs={{0,1},{1,0},{2,3},{3,2},{4,5},{5,4},{6,7},{7,6},{8,9},{9,8},{10,11... | collective-permute-start | bytes 1769480 | tf_op jit(solution)/shard_map/ppermute | solution.py:23
  382.3 22.2 %collective-permute-start.6 = (bf16[192,2304]{1,0:T(8,128)(2,1)}, bf16[192,2304]{1,0:T(8,128)(2,1)}, u32[]{:S(2)}, u32[]{:S(2)}) collective-permute-start(bf16[192,2304]{1,0:T(8,128)(2,1)} %constant_dynamic-slice_fusion.16), channel_id=1, source_target_pairs={{0,2},{1,3},{2,0},{3,1},{4,6},{5,7},{6,4},{7,5},{8,10},{9,11},{10,... | collective-permute-start | bytes 2654216 | tf_op jit(solution)/shard_map/ppermute | solution.py:23
  385.5 44.0 %collective-permute-start.33 = (bf16[1536,768]{1,0:T(8,128)(2,1)}, bf16[1536,768]{1,0:T(8,128)(2,1)}, u32[]{:S(2)}, u32[]{:S(2)}) collective-permute-start(bf16[1536,768]{1,0:T(8,128)(2,1)} %constant_dynamic-slice_fusion.5), channel_id=1, source_target_pairs={{0,1},{1,0},{2,3},{3,2},{4,5},{5,4},{6,7},{7,6},{8,9},{9,8},{10,11... | collective-permute-start | bytes 7077896 | tf_op jit(solution)/shard_map/ppermute | solution.py:23
  406.1 11.7 %collective-permute-start.7 = (bf16[96,2304]{1,0:T(8,128)(2,1)S(1)}, bf16[96,2304]{1,0:T(8,128)(2,1)S(1)}, u32[]{:S(2)}, u32[]{:S(2)}) collective-permute-start(bf16[96,2304]{1,0:T(8,128)(2,1)S(1)} %constant_dynamic-slice_fusion.15), channel_id=1, source_target_pairs={{0,4},{1,5},{2,6},{3,7},{4,0},{5,1},{6,2},{7,3},{8,12},{9,13},{10,... | collective-permute-start | bytes 1327112 | tf_op jit(solution)/shard_map/ppermute | solution.py:23
  417.9 11.4 %collective-permute-start.8 = (bf16[48,2304]{1,0:T(8,128)(2,1)S(1)}, bf16[48,2304]{1,0:T(8,128)(2,1)S(1)}, u32[]{:S(2)}, u32[]{:S(2)}) collective-permute-start(bf16[48,2304]{1,0:T(8,128)(2,1)S(1)} %constant_dynamic-slice_fusion.14), channel_id=1, source_target_pairs={{0,8},{1,9},{2,10},{3,11},{4,12},{5,13},{6,14},{7,15},{8,0},{9,1},... | collective-permute-start | bytes 663560 | tf_op jit(solution)/shard_map/ppermute | solution.py:23
  418.1 29.0 %collective-permute-start.26 = (bf16[192,3072]{1,0:T(8,128)(2,1)S(1)}, bf16[192,3072]{1,0:T(8,128)(2,1)S(1)}, u32[]{:S(2)}, u32[]{:S(2)}) collective-permute-start(bf16[192,3072]{1,0:T(8,128)(2,1)S(1)} %constant_dynamic-slice_fusion.8), channel_id=1, source_target_pairs={{0,2},{1,3},{2,0},{3,1},{4,6},{5,7},{6,4},{7,5},{8,10},{9,11},{10,... | collective-permute-start | bytes 3538952 | tf_op jit(solution)/shard_map/ppermute | solution.py:23
  429.4 10.3 %collective-permute-start.9 = (bf16[48,2304]{1,0:T(8,128)(2,1)S(1)}, bf16[48,2304]{1,0:T(8,128)(2,1)S(1)}, u32[]{:S(2)}, u32[]{:S(2)}) collective-permute-start(bf16[48,2304]{1,0:T(8,128)(2,1)S(1)} %add_convert_fusion.17), channel_id=1, source_target_pairs={{0,8},{1,9},{2,10},{3,11},{4,12},{5,13},{6,14},{7,15},{8,0},{9,1},... | collective-permute-start | bytes 663560 | tf_op jit(solution)/shard_map/ppermute | solution.py:23
  431.9 38.1 %collective-permute-start.34 = (bf16[768,768]{1,0:T(8,128)(2,1)S(1)}, bf16[768,768]{1,0:T(8,128)(2,1)S(1)}, u32[]{:S(2)}, u32[]{:S(2)}) collective-permute-start(bf16[768,768]{1,0:T(8,128)(2,1)S(1)} %constant_dynamic-slice_fusion.4), channel_id=1, source_target_pairs={{0,2},{1,3},{2,0},{3,1},{4,6},{5,7},{6,4},{7,5},{8,10},{9,11},{10,... | collective-permute-start | bytes 3538952 | tf_op jit(solution)/shard_map/ppermute | solution.py:23
  447.5 23.6 %collective-permute-start.27 = (bf16[96,3072]{1,0:T(8,128)(2,1)S(1)}, bf16[96,3072]{1,0:T(8,128)(2,1)S(1)}, u32[]{:S(2)}, u32[]{:S(2)}) collective-permute-start(bf16[96,3072]{1,0:T(8,128)(2,1)S(1)} %constant_dynamic-slice_fusion.7), channel_id=1, source_target_pairs={{0,4},{1,5},{2,6},{3,7},{4,0},{5,1},{6,2},{7,3},{8,12},{9,13},{10,... | collective-permute-start | bytes 1769480 | tf_op jit(solution)/shard_map/ppermute | solution.py:23
  448.6 41.5 %collective-permute-start.10 = (bf16[96,2304]{1,0:T(8,128)(2,1)S(1)}, bf16[96,2304]{1,0:T(8,128)(2,1)S(1)}, u32[]{:S(2)}, u32[]{:S(2)}) collective-permute-start(bf16[96,2304]{1,0:T(8,128)(2,1)S(1)} %pad_maximum_fusion.11), channel_id=1, source_target_pairs={{0,4},{1,5},{2,6},{3,7},{4,0},{5,1},{6,2},{7,3},{8,12},{9,13},{10,... | collective-permute-start | bytes 1327112 | tf_op jit(solution)/shard_map/ppermute | solution.py:23
  470.3 19.3 %collective-permute-start.35 = (bf16[384,768]{1,0:T(8,128)(2,1)S(1)}, bf16[384,768]{1,0:T(8,128)(2,1)S(1)}, u32[]{:S(2)}, u32[]{:S(2)}) collective-permute-start(bf16[384,768]{1,0:T(8,128)(2,1)S(1)} %constant_dynamic-slice_fusion.3), channel_id=1, source_target_pairs={{0,4},{1,5},{2,6},{3,7},{4,0},{5,1},{6,2},{7,3},{8,12},{9,13},{10,... | collective-permute-start | bytes 1769480 | tf_op jit(solution)/shard_map/ppermute | solution.py:23
  471.3 33.0 %collective-permute-start.28 = (bf16[48,3072]{1,0:T(8,128)(2,1)S(1)}, bf16[48,3072]{1,0:T(8,128)(2,1)S(1)}, u32[]{:S(2)}, u32[]{:S(2)}) collective-permute-start(bf16[48,3072]{1,0:T(8,128)(2,1)S(1)} %constant_dynamic-slice_fusion.6), channel_id=1, source_target_pairs={{0,8},{1,9},{2,10},{3,11},{4,12},{5,13},{6,14},{7,15},{8,0},{9,1},... | collective-permute-start | bytes 884744 | tf_op jit(solution)/shard_map/ppermute | solution.py:23
  489.8 14.2 %collective-permute-start.36 = (bf16[192,768]{1,0:T(8,128)(2,1)S(1)}, bf16[192,768]{1,0:T(8,128)(2,1)S(1)}, u32[]{:S(2)}, u32[]{:S(2)}) collective-permute-start(bf16[192,768]{1,0:T(8,128)(2,1)S(1)} %constant_dynamic-slice_fusion.2), channel_id=1, source_target_pairs={{0,8},{1,9},{2,10},{3,11},{4,12},{5,13},{6,14},{7,15},{8,0},{9,1},... | collective-permute-start | bytes 884744 | tf_op jit(solution)/shard_map/ppermute | solution.py:23
  504.1 21.0 %collective-permute-start.37 = (bf16[192,768]{1,0:T(8,128)(2,1)S(1)}, bf16[192,768]{1,0:T(8,128)(2,1)S(1)}, u32[]{:S(2)}, u32[]{:S(2)}) collective-permute-start(bf16[192,768]{1,0:T(8,128)(2,1)S(1)} %add_convert_fusion.14), channel_id=1, source_target_pairs={{0,8},{1,9},{2,10},{3,11},{4,12},{5,13},{6,14},{7,15},{8,0},{9,1},... | collective-permute-start | bytes 884744 | tf_op jit(solution)/shard_map/ppermute | solution.py:23
  504.3 27.1 %collective-permute-start.29 = (bf16[48,3072]{1,0:T(8,128)(2,1)S(1)}, bf16[48,3072]{1,0:T(8,128)(2,1)S(1)}, u32[]{:S(2)}, u32[]{:S(2)}) collective-permute-start(bf16[48,3072]{1,0:T(8,128)(2,1)S(1)} %add_convert_fusion.15), channel_id=1, source_target_pairs={{0,8},{1,9},{2,10},{3,11},{4,12},{5,13},{6,14},{7,15},{8,0},{9,1},... | collective-permute-start | bytes 884744 | tf_op jit(solution)/shard_map/ppermute | solution.py:23
  525.2 18.9 %collective-permute-start.38 = (bf16[384,768]{1,0:T(8,128)(2,1)S(1)}, bf16[384,768]{1,0:T(8,128)(2,1)S(1)}, u32[]{:S(2)}, u32[]{:S(2)}) collective-permute-start(bf16[384,768]{1,0:T(8,128)(2,1)S(1)} %pad_maximum_fusion.9), channel_id=1, source_target_pairs={{0,4},{1,5},{2,6},{3,7},{4,0},{5,1},{6,2},{7,3},{8,12},{9,13},{10,... | collective-permute-start | bytes 1769480 | tf_op jit(solution)/shard_map/ppermute | solution.py:23
  531.5 25.1 %collective-permute-start.30 = (bf16[96,3072]{1,0:T(8,128)(2,1)S(1)}, bf16[96,3072]{1,0:T(8,128)(2,1)S(1)}, u32[]{:S(2)}, u32[]{:S(2)}) collective-permute-start(bf16[96,3072]{1,0:T(8,128)(2,1)S(1)} %pad_maximum_fusion.8), channel_id=1, source_target_pairs={{0,4},{1,5},{2,6},{3,7},{4,0},{5,1},{6,2},{7,3},{8,12},{9,13},{10,... | collective-permute-start | bytes 1769480 | tf_op jit(solution)/shard_map/ppermute | solution.py:23
  531.7 26.9 %collective-permute-start.11 = (bf16[192,2304]{1,0:T(8,128)(2,1)S(1)}, bf16[192,2304]{1,0:T(8,128)(2,1)S(1)}, u32[]{:S(2)}, u32[]{:S(2)}) collective-permute-start(bf16[192,2304]{1,0:T(8,128)(2,1)S(1)} %pad_maximum_fusion.6), channel_id=1, source_target_pairs={{0,2},{1,3},{2,0},{3,1},{4,6},{5,7},{6,4},{7,5},{8,10},{9,11},{10,... | collective-permute-start | bytes 2654216 | tf_op jit(solution)/shard_map/ppermute | solution.py:23
  544.4 35.2 %collective-permute-start.39 = (bf16[768,768]{1,0:T(8,128)(2,1)S(1)}, bf16[768,768]{1,0:T(8,128)(2,1)S(1)}, u32[]{:S(2)}, u32[]{:S(2)}) collective-permute-start(bf16[768,768]{1,0:T(8,128)(2,1)S(1)} %pad_maximum_fusion.5), channel_id=1, source_target_pairs={{0,2},{1,3},{2,0},{3,1},{4,6},{5,7},{6,4},{7,5},{8,10},{9,11},{10,... | collective-permute-start | bytes 3538952 | tf_op jit(solution)/shard_map/ppermute | solution.py:23
  556.9 46.9 %collective-permute-start.31 = (bf16[192,3072]{1,0:T(8,128)(2,1)S(1)}, bf16[192,3072]{1,0:T(8,128)(2,1)S(1)}, u32[]{:S(2)}, u32[]{:S(2)}) collective-permute-start(bf16[192,3072]{1,0:T(8,128)(2,1)S(1)} %pad_maximum_fusion.4), channel_id=1, source_target_pairs={{0,2},{1,3},{2,0},{3,1},{4,6},{5,7},{6,4},{7,5},{8,10},{9,11},{10,... | collective-permute-start | bytes 3538952 | tf_op jit(solution)/shard_map/ppermute | solution.py:23
  559.0 45.7 %collective-permute-start.12 = (bf16[384,2304]{1,0:T(8,128)(2,1)S(1)}, bf16[384,2304]{1,0:T(8,128)(2,1)S(1)}, u32[]{:S(2)}, u32[]{:S(2)}) collective-permute-start(bf16[384,2304]{1,0:T(8,128)(2,1)S(1)} %pad_maximum_fusion.3), channel_id=1, source_target_pairs={{0,1},{1,0},{2,3},{3,2},{4,5},{5,4},{6,7},{7,6},{8,9},{9,8},{10,11... | collective-permute-start | bytes 5308424 | tf_op jit(solution)/shard_map/ppermute | solution.py:23
  580.2 28.7 %collective-permute-start.40 = (bf16[1536,768]{1,0:T(8,128)(2,1)S(1)}, bf16[1536,768]{1,0:T(8,128)(2,1)S(1)}, u32[]{:S(2)}, u32[]{:S(2)}) collective-permute-start(bf16[1536,768]{1,0:T(8,128)(2,1)S(1)} %pad_maximum_fusion.2), channel_id=1, source_target_pairs={{0,1},{1,0},{2,3},{3,2},{4,5},{5,4},{6,7},{7,6},{8,9},{9,8},{10,11... | collective-permute-start | bytes 7077896 | tf_op jit(solution)/shard_map/ppermute | solution.py:23
  604.6 9.8 %collective-permute-start.32 = (bf16[384,3072]{1,0:T(8,128)(2,1)S(1)}, bf16[384,3072]{1,0:T(8,128)(2,1)S(1)}, u32[]{:S(2)}, u32[]{:S(2)}) collective-permute-start(bf16[384,3072]{1,0:T(8,128)(2,1)S(1)} %pad_maximum_fusion.1), channel_id=1, source_target_pairs={{0,1},{1,0},{2,3},{3,2},{4,5},{5,4},{6,7},{7,6},{8,9},{9,8},{10,11... | collective-permute-start | bytes 7077896 | tf_op jit(solution)/shard_map/ppermute | solution.py:23
  (107 other events, 829.1 us)
